TPU v7x, 256 devices: a whole 4x4x8 slice. The times are simulated.
256 devices in a mesh: term: 8 (over z), sector: 32 (over y, x, core).
Axes of the slice: x: 4, y: 4, z: 8, core: 2. Of those that a mesh axis runs over, the one named last changes fastest.
Arguments:
- left_ops: float32 [8, 32, 512, 512], P('term', 'sector'), may hold values from -1 to 2, as said below
- right_ops: float32 [8, 32, 512, 512], P('term', 'sector'), may hold values from -1 to 2, as said below
- hop_left: float32 [8, 32, 512, 512], P('term', 'sector'), may hold values from -0.0625 to 0.0625
- hop_right: float32 [8, 32, 512, 512], P('term', 'sector'), may hold values from -0.0625 to 0.0625
- v_left: bfloat16 [8, 32, 512, 128], P('term', 'sector'), may hold values from -0.5 to 0.5
- v_right: bfloat16 [8, 32, 128, 512], P('term', 'sector'), may hold values from -1.5 to 1.5
- zero_blocks: bfloat16 [32, 128, 128], P('sector'), may hold values from -6 to 6
- links: int32 [8, 32], P('term', 'sector'), may hold values from 0 to 31
- block_dims: int32 [32], P('sector'), may hold values from 128 to 512
Outputs:
- solution: float32 [32, 512, 512], P('sector')
- residual: float32 [32, 512, 512], P('sector')
Inputs may be any that keep to these rules, and one draw needn't show every extreme that they name: Every block left_ops[t, s] and right_ops[t, s] is symmetric and positive definite. `right_ops`: every block is symmetric and positive definite.
All inputs are finite; a program needn't handle non-finite values.
Results may differ from a plain program's by a relative error of at most 0.0003.
Values may be sent and summed in bfloat16 or wider, within the bound.
No kernel may reach another device: no remote copies, remote signals or barrier semaphores. Data moves between devices by JAX's collectives and lax.ppermute only.
A program may use at most 64 MiB of HBM per device.

v0:
```python
import jax
import jax.numpy as jnp
from jax import lax
from jax.sharding import Mesh
from jax.sharding import PartitionSpec as P

ITERS = 3
SECTOR = ("sector_0", "sector_1", "sector_2")
TERM_SECTOR = ("term", "sector_0", "sector_1", "sector_2")
level_gap = 2.5
exact = lax.Precision.HIGHEST


def shifted(value, axis, steps):
    count = lax.axis_size(axis)
    first, last = (max(0, -steps), min(count, count - steps))
    return lax.ppermute(value, axis, [(source, source + steps) for source in range(first, last)])


def copy_for_each(array, axis):
    size = lax.axis_size(axis)
    return lax.all_to_all(
        jnp.broadcast_to(array[None], (size, *array.shape)), axis, 0, 0, tiled=True
    )


def in_order(tiles, dim):
    shape = list(tiles.shape[1:])
    shape[dim] *= tiles.shape[0]
    return jnp.moveaxis(tiles, 0, dim).reshape(shape)


def gathered_copies(array, axis, dim):
    tiles = copy_for_each(array, axis)
    return in_order(tiles, dim)


def in_blocks(array, dim, size):
    shape = array.shape
    tiles = array.reshape(*shape[:dim], size, shape[dim] // size, *shape[dim + 1 :])
    return jnp.moveaxis(tiles, dim, 0)


def summed_on_arrival(array, axis, dim):
    tiles = in_blocks(array, dim, lax.axis_size(axis))
    arrived = lax.all_to_all(tiles, axis, split_axis=0, concat_axis=0, tiled=True)
    return arrived.sum(axis=0)


def one_axis_at_a_time(array, axes):
    for axis in axes:
        array = lax.psum(array, axis)
    return array


def sent_together(arrays, axis, dim, along):
    both = jnp.concatenate(arrays, axis=along)
    out, at, finished = (lax.all_gather(both, axis, axis=dim, tiled=True), 0, [])
    for a in arrays:
        finished.append(lax.slice_in_dim(out, at, at + a.shape[along], axis=along))
        at += a.shape[along]
    return tuple(finished)


def apply_terms(field, left_op, right_op, hop_in, hop_out):
    behind = jnp.einsum("tji,jk->tik", hop_in, field, precision=exact)
    handed = jnp.einsum("tik,tlk->il", behind, hop_out, precision=exact)
    arrived = shifted(handed, SECTOR, 1)
    after = shifted(field, SECTOR, -1)
    inner_part = jnp.einsum("tij,jk->tik", left_op, field, precision=exact)
    running = jnp.einsum("tik,tkl->il", inner_part, right_op, precision=exact)
    ahead = jnp.einsum("tij,jk->tik", hop_in, after, precision=exact)
    running = running + jnp.einsum("tik,tkl->il", ahead, hop_out, precision=exact)
    return running + arrived


def body(left_ops, right_ops, hop_left, hop_right, v_left, v_right, zero_blocks, links, block_dims):
    width = left_ops.shape[-1]
    share = width // lax.axis_size("term")
    offset = lax.axis_index("term") * share
    positions = lax.iota(jnp.int32, width)
    live = positions < block_dims[0]
    live_mask = jnp.logical_and(live[:, None], live[None, :]).astype(jnp.float32)
    left_op = left_ops[:, 0]
    right_op = right_ops[:, 0]
    hop_in = hop_left[:, 0]
    hop_out = hop_right[:, 0]
    everyone = gathered_copies(zero_blocks, SECTOR, 0)
    picked = everyone[links[:, 0]]
    middle = jnp.einsum("tij,tjk->tik", v_left[:, 0], picked, preferred_element_type=jnp.float32)
    source_part = jnp.einsum(
        "tik,tkl->il", middle, v_right[:, 0].astype(jnp.float32), precision=exact
    )
    local_mask = lax.dynamic_slice_in_dim(live_mask, offset, share, 0)
    source = -local_mask * summed_on_arrival(source_part, "term", 0)

    def operate(vector):
        whole_rows = lax.all_gather(vector, "term", axis=0, tiled=True)
        summed = summed_on_arrival(
            apply_terms(whole_rows, left_op, right_op, hop_in, hop_out), "term", 0
        )
        return local_mask * (level_gap * vector + summed)

    def own_rows(product):
        return jnp.sum(product)

    def paired(vector, image_vec):
        return (
            one_axis_at_a_time(own_rows(vector * vector), TERM_SECTOR),
            one_axis_at_a_time(own_rows(vector * image_vec), TERM_SECTOR),
        )

    solution = jnp.zeros_like(source)
    residual = source
    image_vec = operate(residual)
    norm_now, product = paired(residual, image_vec)
    step_size = norm_now / product
    direction = residual
    along = image_vec
    for sweep_index in range(ITERS):
        solution = solution + step_size * direction
        residual = residual - step_size * along
        if sweep_index + 1 < ITERS:
            image_vec = operate(residual)
            norm_next, product = paired(residual, image_vec)
            ratio = norm_next / norm_now
            step_size = norm_next / (product - ratio * norm_next / step_size)
            direction = residual + ratio * direction
            along = image_vec + ratio * along
            norm_now = norm_next
    solution, residual = sent_together((solution, residual), "term", 0, 1)
    return (solution[None], residual[None])


def solution(mesh):
    finer = Mesh(
        mesh.devices.reshape(mesh.shape["term"], 4, 4, 2),
        ("term", "sector_0", "sector_1", "sector_2"),
    )
    in_specs = (
        P("term", SECTOR, None, None),
        P("term", SECTOR, None, None),
        P("term", SECTOR, None, None),
        P("term", SECTOR, None, None),
        P("term", SECTOR, None, None),
        P("term", SECTOR, None, None),
        P(SECTOR, None, None),
        P("term", SECTOR),
        P(SECTOR),
    )
    out_specs = (P(SECTOR, None, None), P(SECTOR, None, None))
    return jax.shard_map(body, mesh=finer, in_specs=in_specs, out_specs=out_specs, check_vma=False)
```

profile of v0, /device:TPU:2, one launch (start us, length us, event | category | flops | bytes accessed | tf_op | source)
XLA Modules:
  0.0 529.2 jit_solution(18221655334266189358)
XLA Ops:
  9.3 7.6 %all-to-all-start = ((bf16[32,1,128,128]{3,2,1,0:T(8,128)(2,1)}), bf16[32,1,128,128]{3,2,1,0:T(8,128)(2,1)S(1)}, u32[]{:S(2)}, u32[]{:S(2)}) async-start(bf16[32,1,128,128]{3,2,1,0:T(8,128)(2,1)} %broadcast_in_dim.20), calls=%async_computation | async-start | bytes 2097152 | tf_op jit(solution)/shard_map/all_to_all | solution.py:22
  17.5 15.3 %all-to-all-done = bf16[32,1,128,128]{3,2,1,0:T(8,128)(2,1)S(1)} async-done(((bf16[32,1,128,128]{3,2,1,0:T(8,128)(2,1)}), bf16[32,1,128,128]{3,2,1,0:T(8,128)(2,1)S(1)}, u32[]{:S(2)}, u32[]{:S(2)}) %all-to-all-start) | async-done | bytes 1048608 | tf_op jit(solution)/shard_map/all_to_all | solution.py:22
  34.8 8.5 %all-to-all-start.1 = ((f32[8,64,512]{2,1,0:T(8,128)}), f32[8,64,512]{2,1,0:T(8,128)S(1)}, u32[]{:S(2)}, u32[]{:S(2)}) async-start(f32[8,64,512]{2,1,0:T(8,128)} %fusion.37), calls=%async_computation.1 | async-start | bytes 2097152 | tf_op jit(solution)/shard_map/all_to_all | solution.py:46
  44.0 28.4 %all-to-all-done.1 = f32[8,64,512]{2,1,0:T(8,128)S(1)} async-done(((f32[8,64,512]{2,1,0:T(8,128)}), f32[8,64,512]{2,1,0:T(8,128)S(1)}, u32[]{:S(2)}, u32[]{:S(2)}) %all-to-all-start.1) | async-done | bytes 1048608 | tf_op jit(solution)/shard_map/all_to_all | solution.py:46
  73.4 32.3 %all-gather.5.cloned.1.call-done = f32[512,512]{1,0:T(8,128)} async-done(((f32[64,512]{1,0:T(8,128)}), f32[512,512]{1,0:T(8,128)}) %all-gather.5.cloned.1.call-update) | async-done | bytes 1048592 | tf_op jit(solution)/shard_map/all_gather | solution.py:98
  122.4 3.6 fusion.22
  125.9 4.5 collective-permute-done.1
  132.4 32.0 %all_to_all.25 = f32[8,64,512]{2,1,0:T(8,128)} all-to-all(f32[8,64,512]{2,1,0:T(8,128)S(1)} %bitcast.88), channel_id=1, replica_groups=mesh['term'=8,'sector_0'=4,'sector_1'=4,'sector_2'=2] {'term'}, dimensions={0} | all-to-all | bytes 2097152 | tf_op jit(solution)/shard_map/all_to_all | solution.py:46
  166.4 15.3 %all-reduce.2 = (f32[]{:T(128)}, f32[]{:T(128)}) all-reduce(f32[]{:T(128)} %get-tuple-element.18, f32[]{:T(128)} %get-tuple-element.17), channel_id=1, replica_groups=mesh['term'=8,'sector_0'=4,'sector_1'=4,'sector_2'=2] {'term'}, use_global_device_ids=true, to_apply=%region_2.0 | all-reduce | flops 2 | bytes 16 | tf_op jit(solution)/shard_map/psum | solution.py:52
  181.8 11.1 %all-reduce.8 = (f32[]{:T(128)}, f32[]{:T(128)}) all-reduce(f32[]{:T(128)} %get-tuple-element.23, f32[]{:T(128)} %get-tuple-element.24), channel_id=1, replica_groups=mesh['term'=8,'sector_0'=4,'sector_1'=4,'sector_2'=2] {'sector_0'}, use_global_device_ids=true, to_apply=%region_3.0 | all-reduce | flops 2 | bytes 16 | tf_op jit(solution)/shard_map/psum | solution.py:52
  192.8 8.9 %all-reduce.5 = (f32[]{:T(128)}, f32[]{:T(128)}) all-reduce(f32[]{:T(128)} %get-tuple-element.35, f32[]{:T(128)} %get-tuple-element.36), channel_id=1, replica_groups=mesh['term'=8,'sector_0'=4,'sector_1'=4,'sector_2'=2] {'sector_1'}, use_global_device_ids=true, to_apply=%region_4.0 | all-reduce | flops 2 | bytes 16 | tf_op jit(solution)/shard_map/psum | solution.py:52
  207.0 33.1 %all-gather.7.cloned.1.call-done = f32[512,512]{1,0:T(8,128)} async-done(((f32[64,512]{1,0:T(8,128)}), f32[512,512]{1,0:T(8,128)}) %all-gather.7.cloned.1.call-update) | async-done | bytes 1048592 | tf_op jit(solution)/shard_map/all_gather | solution.py:98
  260.6 4.7 collective-permute-done.3
  267.3 32.1 %all_to_all.26 = f32[8,64,512]{2,1,0:T(8,128)} all-to-all(f32[8,64,512]{2,1,0:T(8,128)S(1)} %bitcast.89), channel_id=1, replica_groups=mesh['term'=8,'sector_0'=4,'sector_1'=4,'sector_2'=2] {'term'}, dimensions={0} | all-to-all | bytes 2097152 | tf_op jit(solution)/shard_map/all_to_all | solution.py:46
  303.0 15.4 %all-reduce.1 = (f32[]{:T(128)}, f32[]{:T(128)}) all-reduce(f32[]{:T(128)} %get-tuple-element.16, f32[]{:T(128)} %get-tuple-element.15), channel_id=1, replica_groups=mesh['term'=8,'sector_0'=4,'sector_1'=4,'sector_2'=2] {'term'}, use_global_device_ids=true, to_apply=%region_13.0 | all-reduce | flops 2 | bytes 16 | tf_op jit(solution)/shard_map/psum | solution.py:52
  318.4 11.1 %all-reduce.7 = (f32[]{:T(128)}, f32[]{:T(128)}) all-reduce(f32[]{:T(128)} %get-tuple-element.21, f32[]{:T(128)} %get-tuple-element.22), channel_id=1, replica_groups=mesh['term'=8,'sector_0'=4,'sector_1'=4,'sector_2'=2] {'sector_0'}, use_global_device_ids=true, to_apply=%region_14.0 | all-reduce | flops 2 | bytes 16 | tf_op jit(solution)/shard_map/psum | solution.py:52
  329.5 9.0 %all-reduce.4 = (f32[]{:T(128)}, f32[]{:T(128)}) all-reduce(f32[]{:T(128)} %get-tuple-element.33, f32[]{:T(128)} %get-tuple-element.34), channel_id=1, replica_groups=mesh['term'=8,'sector_0'=4,'sector_1'=4,'sector_2'=2] {'sector_1'}, use_global_device_ids=true, to_apply=%region_15.0 | all-reduce | flops 2 | bytes 16 | tf_op jit(solution)/shard_map/psum | solution.py:52
  348.1 33.0 %all-gather.9.cloned.1.call-done = f32[512,512]{1,0:T(8,128)} async-done(((f32[64,512]{1,0:T(8,128)}), f32[512,512]{1,0:T(8,128)}) %all-gather.9.cloned.1.call-update) | async-done | bytes 1048592 | tf_op jit(solution)/shard_map/all_gather | solution.py:98
  402.0 3.9 collective-permute-done.5
  407.9 32.0 %all_to_all.27 = f32[8,64,512]{2,1,0:T(8,128)S(1)} all-to-all(f32[8,64,512]{2,1,0:T(8,128)S(1)} %bitcast.90), channel_id=1, replica_groups=mesh['term'=8,'sector_0'=4,'sector_1'=4,'sector_2'=2] {'term'}, dimensions={0} | all-to-all | bytes 2097152 | tf_op jit(solution)/shard_map/all_to_all | solution.py:46
  440.7 15.4 %all-reduce = (f32[]{:T(128)}, f32[]{:T(128)}) all-reduce(f32[]{:T(128)} %get-tuple-element.14, f32[]{:T(128)} %get-tuple-element.13), channel_id=1, replica_groups=mesh['term'=8,'sector_0'=4,'sector_1'=4,'sector_2'=2] {'term'}, use_global_device_ids=true, to_apply=%region_24.0 | all-reduce | flops 2 | bytes 16 | tf_op jit(solution)/shard_map/psum | solution.py:52
  456.1 11.1 %all-reduce.6 = (f32[]{:T(128)}, f32[]{:T(128)}) all-reduce(f32[]{:T(128)} %get-tuple-element.19, f32[]{:T(128)} %get-tuple-element.20), channel_id=1, replica_groups=mesh['term'=8,'sector_0'=4,'sector_1'=4,'sector_2'=2] {'sector_0'}, use_global_device_ids=true, to_apply=%region_25.0 | all-reduce | flops 2 | bytes 16 | tf_op jit(solution)/shard_map/psum | solution.py:52
  467.2 9.0 %all-reduce.3 = (f32[]{:T(128)}, f32[]{:T(128)}) all-reduce(f32[]{:T(128)} %get-tuple-element.31, f32[]{:T(128)} %get-tuple-element.32), channel_id=1, replica_groups=mesh['term'=8,'sector_0'=4,'sector_1'=4,'sector_2'=2] {'sector_1'}, use_global_device_ids=true, to_apply=%region_26.0 | all-reduce | flops 2 | bytes 16 | tf_op jit(solution)/shard_map/psum | solution.py:52
  483.9 35.6 %all-gather.11.cloned.1.call-done = f32[512,1024]{1,0:T(8,128)} async-done(((f32[64,1024]{1,0:T(8,128)}), f32[512,1024]{1,0:T(8,128)}) %all-gather.11.cloned.1.call-update) | async-done | bytes 2097168 | tf_op jit(solution)/shard_map/all_gather | solution.py:58
  (84 shorter events, 91.0 us)
Async XLA Ops:
  7.2 100.4 %copy-start = (f32[1,1,512,512]{3,2,1,0:T(8,128)S(1)}, f32[1,1,512,512]{3,2,1,0:T(8,128)}, u32[]{:S(2)}) copy-start(f32[1,1,512,512]{3,2,1,0:T(8,128)} %param.11) | copy-start | bytes 3145732
  7.2 25.7 %copy-start.12 = (bf16[1,1,512,128]{3,2,1,0:T(8,128)(2,1)S(1)}, bf16[1,1,512,128]{3,2,1,0:T(8,128)(2,1)}, u32[]{:S(2)}) copy-start(bf16[1,1,512,128]{3,2,1,0:T(8,128)(2,1)} %param.13) | copy-start | bytes 393220
  7.2 26.0 %copy-start.13 = (bf16[1,1,128,512]{3,2,1,0:T(8,128)(2,1)S(1)}, bf16[1,1,128,512]{3,2,1,0:T(8,128)(2,1)}, u32[]{:S(2)}) copy-start(bf16[1,1,128,512]{3,2,1,0:T(8,128)(2,1)} %param.14) | copy-start | bytes 393220
  9.3 23.6 %all-to-all-start = ((bf16[32,1,128,128]{3,2,1,0:T(8,128)(2,1)}), bf16[32,1,128,128]{3,2,1,0:T(8,128)(2,1)S(1)}, u32[]{:S(2)}, u32[]{:S(2)}) async-start(bf16[32,1,128,128]{3,2,1,0:T(8,128)(2,1)} %broadcast_in_dim.20), calls=%async_computation | async-start | bytes 2097152 | tf_op jit(solution)/shard_map/all_to_all | solution.py:22
  34.8 37.7 %all-to-all-start.1 = ((f32[8,64,512]{2,1,0:T(8,128)}), f32[8,64,512]{2,1,0:T(8,128)S(1)}, u32[]{:S(2)}, u32[]{:S(2)}) async-start(f32[8,64,512]{2,1,0:T(8,128)} %fusion.37), calls=%async_computation.1 | async-start | bytes 2097152 | tf_op jit(solution)/shard_map/all_to_all | solution.py:46
  43.2 62.4 %all-gather.5.cloned.1.call-start = ((), (), s32[]{:S(2)}) async-start(), calls=%async_computation.5 | async-start | bytes 1179648 | tf_op jit(solution)/shard_map/all_gather | solution.py:98
  44.0 66.6 %copy-start.1 = (f32[1,1,512,512]{3,2,1,0:T(8,128)S(1)}, f32[1,1,512,512]{3,2,1,0:T(8,128)}, u32[]{:S(2)}) copy-start(f32[1,1,512,512]{3,2,1,0:T(8,128)} %param.12) | copy-start | bytes 3145732
  73.3 166.8 %all-gather.7.cloned.1.call-start = ((), (), s32[]{:S(2)}) async-start(), calls=%async_computation.6 | async-start | bytes 1179648 | tf_op jit(solution)/shard_map/all_gather | solution.py:98
  105.7 16.7 %collective-permute-start = (f32[512,512]{1,0:T(8,128)}, f32[512,512]{1,0:T(8,128)S(1)}, u32[]{:S(2)}, u32[]{:S(2)}) collective-permute-start(f32[512,512]{1,0:T(8,128)} %all-gather.5.cloned.1.call-done), channel_id=1, source_target_pairs={{1,0},{2,1},{3,2},{4,3},{5,4},{6,5},{7,6},{8,7},{9,8},{10,9},{11,1... | collective-permute-start | bytes 3145736 | tf_op jit(solution)/shard_map/ppermute | solution.py:17
  110.7 6.2 %copy-start.2 = (f32[1,1,512,512]{3,2,1,0:T(8,128)S(1)}, f32[1,1,512,512]{3,2,1,0:T(8,128)}, u32[]{:S(2)}) copy-start(f32[1,1,512,512]{3,2,1,0:T(8,128)} %param.9) | copy-start | bytes 3145732
  110.7 6.2 %copy-start.6 = (f32[512,512]{1,0:T(8,128)S(1)}, f32[512,512]{1,0:T(8,128)}, u32[]{:S(2)}) copy-start(f32[512,512]{1,0:T(8,128)} %all-gather.5.cloned.1.call-done) | copy-start | bytes 3145732
  114.2 6.2 %copy-start.3 = (f32[1,1,512,512]{3,2,1,0:T(8,128)S(1)}, f32[1,1,512,512]{3,2,1,0:T(8,128)}, u32[]{:S(2)}) copy-start(f32[1,1,512,512]{3,2,1,0:T(8,128)} %param.10) | copy-start | bytes 3145732
  114.2 16.2 %collective-permute-start.1 = (f32[512,512]{1,0:T(8,128)S(1)}, f32[512,512]{1,0:T(8,128)S(1)}, u32[]{:S(2)}, u32[]{:S(2)}) collective-permute-start(f32[512,512]{1,0:T(8,128)S(1)} %fusion.9), channel_id=1, source_target_pairs={{0,1},{1,2},{2,3},{3,4},{4,5},{5,6},{6,7},{7,8},{8,9},{9,10},{10,1... | collective-permute-start | bytes 3145736 | tf_op jit(solution)/shard_map/ppermute | solution.py:17
  207.0 174.1 %all-gather.9.cloned.1.call-start = ((), (), s32[]{:S(2)}) async-start(), calls=%async_computation.7 | async-start | bytes 1179648 | tf_op jit(solution)/shard_map/all_gather | solution.py:98
  240.2 16.9 %collective-permute-start.2 = (f32[512,512]{1,0:T(8,128)}, f32[512,512]{1,0:T(8,128)S(1)}, u32[]{:S(2)}, u32[]{:S(2)}) collective-permute-start(f32[512,512]{1,0:T(8,128)} %all-gather.7.cloned.1.call-done), channel_id=1, source_target_pairs={{1,0},{2,1},{3,2},{4,3},{5,4},{6,5},{7,6},{8,7},{9,8},{10,9},{11,1... | collective-permute-start | bytes 3145736 | tf_op jit(solution)/shard_map/ppermute | solution.py:17
  245.6 6.1 %copy-start.7 = (f32[512,512]{1,0:T(8,128)S(1)}, f32[512,512]{1,0:T(8,128)}, u32[]{:S(2)}) copy-start(f32[512,512]{1,0:T(8,128)} %all-gather.7.cloned.1.call-done) | copy-start | bytes 3145732
  249.1 6.1 %copy-start.4 = (f32[1,1,512,512]{3,2,1,0:T(8,128)S(1)}, f32[1,1,512,512]{3,2,1,0:T(8,128)}, u32[]{:S(2)}) copy-start(f32[1,1,512,512]{3,2,1,0:T(8,128)} %param.10) | copy-start | bytes 3145732
  249.1 16.2 %collective-permute-start.3 = (f32[512,512]{1,0:T(8,128)S(1)}, f32[512,512]{1,0:T(8,128)S(1)}, u32[]{:S(2)}, u32[]{:S(2)}) collective-permute-start(f32[512,512]{1,0:T(8,128)S(1)} %fusion.6), channel_id=1, source_target_pairs={{0,1},{1,2},{2,3},{3,4},{4,5},{5,6},{6,7},{7,8},{8,9},{9,10},{10,1... | collective-permute-start | bytes 3145736 | tf_op jit(solution)/shard_map/ppermute | solution.py:17
  267.2 34.1 %copy-start.9 = (f32[64,512]{1,0:T(8,128)S(1)}, f32[64,512]{1,0:T(8,128)}, u32[]{:S(2)}) copy-start(f32[64,512]{1,0:T(8,128)} %multiply_subtract_fusion.2) | copy-start | bytes 393220
  347.9 171.6 %all-gather.11.cloned.1.call-start = ((), (), s32[]{:S(2)}) async-start(), calls=%async_computation.8 | async-start | bytes 2359296 | tf_op jit(solution)/shard_map/all_gather | solution.py:58
  384.2 14.2 %collective-permute-start.4 = (f32[512,512]{1,0:T(8,128)S(1)}, f32[512,512]{1,0:T(8,128)S(1)}, u32[]{:S(2)}, u32[]{:S(2)}) collective-permute-start(f32[512,512]{1,0:T(8,128)S(1)} %copy-done.8), channel_id=1, source_target_pairs={{1,0},{2,1},{3,2},{4,3},{5,4},{6,5},{7,6},{8,7},{9,8},{10,9},{11,1... | collective-permute-start | bytes 3145736 | tf_op jit(solution)/shard_map/ppermute | solution.py:17
  389.7 16.2 %collective-permute-start.5 = (f32[512,512]{1,0:T(8,128)S(1)}, f32[512,512]{1,0:T(8,128)S(1)}, u32[]{:S(2)}, u32[]{:S(2)}) collective-permute-start(f32[512,512]{1,0:T(8,128)S(1)} %fusion.3), channel_id=1, source_target_pairs={{0,1},{1,2},{2,3},{3,4},{4,5},{5,6},{6,7},{7,8},{8,9},{9,10},{10,1... | collective-permute-start | bytes 3145736 | tf_op jit(solution)/shard_map/ppermute | solution.py:17
  407.8 32.1 %copy-start.10 = (f32[64,512]{1,0:T(8,128)S(1)}, f32[64,512]{1,0:T(8,128)}, u32[]{:S(2)}) copy-start(f32[64,512]{1,0:T(8,128)} %get-tuple-element.43) | copy-start | bytes 393220
  407.8 75.1 %copy-start.11 = (f32[64,512]{1,0:T(8,128)S(1)}, f32[64,512]{1,0:T(8,128)}, u32[]{:S(2)}) copy-start(f32[64,512]{1,0:T(8,128)} %get-tuple-element.44) | copy-start | bytes 393220
  (2 other events, 9.2 us)
Sparse Core Ops, SparseCore 0:
  73.4 32.1 all-gather.4
  207.1 33.0 all-gather.6
  348.0 33.0 all-gather.8
  484.0 35.4 all-gather.10
where the time goes:
time: 536 us; the launch traced here: 529 us
  blocking collectives  212 us (40%)
  waiting for transfers between devices  192 us (36%)
  matrix products  54 us (10%)
  starting transfers between devices  30.3 us (6%)
  between operations  25.3 us (5%)
  other arithmetic  10.6 us (2%)
  local copies, waits for them, and re-layouts  5.37 us (1%)
    psum x12, blocking collectives, one_axis_at_a_time(): array = lax.psum(array, axis)  116 us
    all_gather x3, waiting for transfers between devices, operate(): whole_rows = lax.all_gather(vector, 'term', axis=0, tiled=True)  98.4 us
    all_to_all x3, blocking collectives, summed_on_arrival(): lax.all_to_all(tiles, axis, split_axis=0, concat_axis=0, tiled=True)  96.2 us
    all_gather x1, waiting for transfers between devices, sent_together(): lax.all_gather(both, axis, axis=dim, tiled=True)  35.6 us
    all_to_all x1, waiting for transfers between devices, summed_on_arrival(): lax.all_to_all(tiles, axis, split_axis=0, concat_axis=0, tiled=True)  28.4 us
    all_to_all x1, waiting for transfers between devices, copy_for_each(): lax.all_to_all(jnp.broadcast_to(array[None], (size, *array.shape)), axis,...  15.3 us
    ppermute x6, waiting for transfers between devices, shifted(): lax.ppermute(value, axis, [(source, source + steps) for source in range(f...  14 us
    ppermute x6, starting transfers between devices, shifted(): lax.ppermute(value, axis, [(source, source + steps) for source in range(f...  13.9 us
  transfers between devices with their start and end apart: 12, of which 10 were waited for; matrix products, arithmetic and copies ran while one was open for 8% of the time, Pallas kernels for 0%

commit v1 on v0

--- a/solution.py
+++ b/solution.py
@@ -95,7 +95,16 @@
     source = -local_mask * summed_on_arrival(source_part, "term", 0)
 
     def operate(vector):
-        whole_rows = lax.all_gather(vector, "term", axis=0, tiled=True)
+        ways = lax.axis_size("term")
+        up = [(d, (d + 1) % ways) for d in range(ways)]
+        down = [(d, (d - 1) % ways) for d in range(ways)]
+        earlier, later = ([vector], [vector])
+        for _ in range(ways // 2):
+            earlier.append(lax.ppermute(earlier[-1], "term", up))
+        for _ in range((ways - 1) // 2):
+            later.append(lax.ppermute(later[-1], "term", down))
+        line = jnp.concatenate([*earlier[::-1], *later[1:]], axis=0)
+        whole_rows = jnp.roll(line, (lax.axis_index("term") - ways // 2) * vector.shape[0], axis=0)
         summed = summed_on_arrival(
             apply_terms(whole_rows, left_op, right_op, hop_in, hop_out), "term", 0
         )

time: 536 us -> 509 us (0.950)
  waiting for transfers between devices: 192 us -> 137 us
  starting transfers between devices: 30.3 us -> 64.5 us
    all_gather x3 -> x0, waiting for transfers between devices: 98.4 us -> none  [operate(): whole_rows = lax.all_gather(vector, 'term', axis=0, tiled=True)]
    ppermute x0 -> x21, waiting for transfers between devices: none -> 43.2 us  [the longest x12 43.2 us: operate(): earlier.append(lax.ppermute(earlier[-1], 'term', up))]
    ppermute x0 -> x21, starting transfers between devices: none -> 33.3 us  [the longest x9 28.6 us: operate(): later.append(lax.ppermute(later[-1], 'term', down))]
  transfers between devices with their start and end apart: 12 -> 30, of which waited for: 10 -> 20; matrix products, arithmetic and copies ran while one was open for 8% -> 8% of each run, Pallas kernels for 0% -> 0%
where the time goes in v1:
time: 509 us; the launch traced here: 502 us
  blocking collectives  208 us (41%)
  waiting for transfers between devices  137 us (27%)
  starting transfers between devices  64.5 us (13%)
  matrix products  49.6 us (10%)
  between operations  26.6 us (5%)
  other arithmetic  10.7 us (2%)
  local copies, waits for them, and re-layouts  5.62 us (1%)
    psum x12, blocking collectives, one_axis_at_a_time(): array = lax.psum(array, axis)  114 us
    all_to_all x3, blocking collectives, summed_on_arrival(): lax.all_to_all(tiles, axis, split_axis=0, concat_axis=0, tiled=True)  93.7 us
    ppermute x12, waiting for transfers between devices, operate(): earlier.append(lax.ppermute(earlier[-1], 'term', up))  43.2 us
    all_gather x1, waiting for transfers between devices, sent_together(): lax.all_gather(both, axis, axis=dim, tiled=True)  35.5 us
    ppermute x9, starting transfers between devices, operate(): later.append(lax.ppermute(later[-1], 'term', down))  28.6 us
    all_to_all x1, waiting for transfers between devices, summed_on_arrival(): lax.all_to_all(tiles, axis, split_axis=0, concat_axis=0, tiled=True)  28.4 us
    all_to_all x1, waiting for transfers between devices, copy_for_each(): lax.all_to_all(jnp.broadcast_to(array[None], (size, *array.shape)), axis,...  15.3 us
    ppermute x6, starting transfers between devices, shifted(): lax.ppermute(value, axis, [(source, source + steps) for source in range(f...  15 us
  transfers between devices with their start and end apart: 30, of which 20 were waited for; matrix products, arithmetic and copies ran while one was open for 8% of the time, Pallas kernels for 0%

profile of v1, /device:TPU:2, one launch (start us, length us, event | category | flops | bytes accessed | tf_op | source)
XLA Modules:
  0.0 502.1 jit_solution(11481362330906064658)
XLA Ops:
  9.3 7.6 %all-to-all-start = ((bf16[32,1,128,128]{3,2,1,0:T(8,128)(2,1)}), bf16[32,1,128,128]{3,2,1,0:T(8,128)(2,1)S(1)}, u32[]{:S(2)}, u32[]{:S(2)}) async-start(bf16[32,1,128,128]{3,2,1,0:T(8,128)(2,1)} %broadcast_in_dim.20), calls=%async_computation | async-start | bytes 2097152 | tf_op jit(solution)/shard_map/all_to_all | solution.py:22
  17.5 15.3 %all-to-all-done = bf16[32,1,128,128]{3,2,1,0:T(8,128)(2,1)S(1)} async-done(((bf16[32,1,128,128]{3,2,1,0:T(8,128)(2,1)}), bf16[32,1,128,128]{3,2,1,0:T(8,128)(2,1)S(1)}, u32[]{:S(2)}, u32[]{:S(2)}) %all-to-all-start) | async-done | bytes 1048608 | tf_op jit(solution)/shard_map/all_to_all | solution.py:22
  34.8 8.5 %all-to-all-start.1 = ((f32[8,64,512]{2,1,0:T(8,128)}), f32[8,64,512]{2,1,0:T(8,128)S(1)}, u32[]{:S(2)}, u32[]{:S(2)}) async-start(f32[8,64,512]{2,1,0:T(8,128)} %fusion.40), calls=%async_computation.1 | async-start | bytes 2097152 | tf_op jit(solution)/shard_map/all_to_all | solution.py:46
  44.0 28.4 %all-to-all-done.1 = f32[8,64,512]{2,1,0:T(8,128)S(1)} async-done(((f32[8,64,512]{2,1,0:T(8,128)}), f32[8,64,512]{2,1,0:T(8,128)S(1)}, u32[]{:S(2)}, u32[]{:S(2)}) %all-to-all-start.1) | async-done | bytes 1048608 | tf_op jit(solution)/shard_map/all_to_all | solution.py:46
  73.2 6.1 %collective-permute-done = f32[64,512]{1,0:T(8,128)S(1)} collective-permute-done((f32[64,512]{1,0:T(8,128)S(1)}, f32[64,512]{1,0:T(8,128)S(1)}, u32[]{:S(2)}, u32[]{:S(2)}) %collective-permute-start) | collective-permute-done | bytes 131104 | tf_op jit(solution)/shard_map/ppermute | solution.py:103
  102.7 3.5 fusion.12
  118.4 4.0 collective-permute-done.8
  124.3 31.2 %all_to_all.25 = f32[8,64,512]{2,1,0:T(8,128)} all-to-all(f32[8,64,512]{2,1,0:T(8,128)S(1)} %bitcast.88), channel_id=1, replica_groups=mesh['term'=8,'sector_0'=4,'sector_1'=4,'sector_2'=2] {'term'}, dimensions={0} | all-to-all | bytes 2097152 | tf_op jit(solution)/shard_map/all_to_all | solution.py:46
  157.6 15.3 %all-reduce.2 = (f32[]{:T(128)}, f32[]{:T(128)}) all-reduce(f32[]{:T(128)} %get-tuple-element.19, f32[]{:T(128)} %get-tuple-element.18), channel_id=1, replica_groups=mesh['term'=8,'sector_0'=4,'sector_1'=4,'sector_2'=2] {'term'}, use_global_device_ids=true, to_apply=%region_2.3 | all-reduce | flops 2 | bytes 16 | tf_op jit(solution)/shard_map/psum | solution.py:52
  172.9 9.4 %all-reduce.8 = (f32[]{:T(128)}, f32[]{:T(128)}) all-reduce(f32[]{:T(128)} %get-tuple-element.24, f32[]{:T(128)} %get-tuple-element.25), channel_id=1, replica_groups=mesh['term'=8,'sector_0'=4,'sector_1'=4,'sector_2'=2] {'sector_0'}, use_global_device_ids=true, to_apply=%region_3.4 | all-reduce | flops 2 | bytes 16 | tf_op jit(solution)/shard_map/psum | solution.py:52
  182.3 10.0 %all-reduce.5 = (f32[]{:T(128)}, f32[]{:T(128)}) all-reduce(f32[]{:T(128)} %get-tuple-element.36, f32[]{:T(128)} %get-tuple-element.37), channel_id=1, replica_groups=mesh['term'=8,'sector_0'=4,'sector_1'=4,'sector_2'=2] {'sector_1'}, use_global_device_ids=true, to_apply=%region_4.5 | all-reduce | flops 2 | bytes 16 | tf_op jit(solution)/shard_map/psum | solution.py:52
  198.5 5.3 %collective-permute-done.9 = f32[64,512]{1,0:T(8,128)S(1)} collective-permute-done((f32[64,512]{1,0:T(8,128)S(1)}, f32[64,512]{1,0:T(8,128)S(1)}, u32[]{:S(2)}, u32[]{:S(2)}) %collective-permute-start.9) | collective-permute-done | bytes 131104 | tf_op jit(solution)/shard_map/ppermute | solution.py:103
  242.9 4.5 collective-permute-done.17
  249.3 31.2 %all_to_all.26 = f32[8,64,512]{2,1,0:T(8,128)} all-to-all(f32[8,64,512]{2,1,0:T(8,128)S(1)} %bitcast.89), channel_id=1, replica_groups=mesh['term'=8,'sector_0'=4,'sector_1'=4,'sector_2'=2] {'term'}, dimensions={0} | all-to-all | bytes 2097152 | tf_op jit(solution)/shard_map/all_to_all | solution.py:46
  284.2 15.4 %all-reduce.1 = (f32[]{:T(128)}, f32[]{:T(128)}) all-reduce(f32[]{:T(128)} %get-tuple-element.17, f32[]{:T(128)} %get-tuple-element.16), channel_id=1, replica_groups=mesh['term'=8,'sector_0'=4,'sector_1'=4,'sector_2'=2] {'term'}, use_global_device_ids=true, to_apply=%region_13.15 | all-reduce | flops 2 | bytes 16 | tf_op jit(solution)/shard_map/psum | solution.py:52
  299.6 9.3 %all-reduce.7 = (f32[]{:T(128)}, f32[]{:T(128)}) all-reduce(f32[]{:T(128)} %get-tuple-element.22, f32[]{:T(128)} %get-tuple-element.23), channel_id=1, replica_groups=mesh['term'=8,'sector_0'=4,'sector_1'=4,'sector_2'=2] {'sector_0'}, use_global_device_ids=true, to_apply=%region_14.16 | all-reduce | flops 2 | bytes 16 | tf_op jit(solution)/shard_map/psum | solution.py:52
  308.8 10.0 %all-reduce.4 = (f32[]{:T(128)}, f32[]{:T(128)}) all-reduce(f32[]{:T(128)} %get-tuple-element.34, f32[]{:T(128)} %get-tuple-element.35), channel_id=1, replica_groups=mesh['term'=8,'sector_0'=4,'sector_1'=4,'sector_2'=2] {'sector_1'}, use_global_device_ids=true, to_apply=%region_15.17 | all-reduce | flops 2 | bytes 16 | tf_op jit(solution)/shard_map/psum | solution.py:52
  330.1 5.3 %collective-permute-done.18 = f32[64,512]{1,0:T(8,128)S(1)} collective-permute-done((f32[64,512]{1,0:T(8,128)S(1)}, f32[64,512]{1,0:T(8,128)S(1)}, u32[]{:S(2)}, u32[]{:S(2)}) %collective-permute-start.18) | collective-permute-done | bytes 131104 | tf_op jit(solution)/shard_map/ppermute | solution.py:103
  374.1 4.6 collective-permute-done.26
  380.5 31.2 %all_to_all.27 = f32[8,64,512]{2,1,0:T(8,128)S(1)} all-to-all(f32[8,64,512]{2,1,0:T(8,128)S(1)} %bitcast.90), channel_id=1, replica_groups=mesh['term'=8,'sector_0'=4,'sector_1'=4,'sector_2'=2] {'term'}, dimensions={0} | all-to-all | bytes 2097152 | tf_op jit(solution)/shard_map/all_to_all | solution.py:46
  412.6 15.3 %all-reduce = (f32[]{:T(128)}, f32[]{:T(128)}) all-reduce(f32[]{:T(128)} %get-tuple-element.15, f32[]{:T(128)} %get-tuple-element.14), channel_id=1, replica_groups=mesh['term'=8,'sector_0'=4,'sector_1'=4,'sector_2'=2] {'term'}, use_global_device_ids=true, to_apply=%region_24.26 | all-reduce | flops 2 | bytes 16 | tf_op jit(solution)/shard_map/psum | solution.py:52
  427.9 10.3 %all-reduce.6 = (f32[]{:T(128)}, f32[]{:T(128)}) all-reduce(f32[]{:T(128)} %get-tuple-element.20, f32[]{:T(128)} %get-tuple-element.21), channel_id=1, replica_groups=mesh['term'=8,'sector_0'=4,'sector_1'=4,'sector_2'=2] {'sector_0'}, use_global_device_ids=true, to_apply=%region_25.27 | all-reduce | flops 2 | bytes 16 | tf_op jit(solution)/shard_map/psum | solution.py:52
  438.3 9.9 %all-reduce.3 = (f32[]{:T(128)}, f32[]{:T(128)}) all-reduce(f32[]{:T(128)} %get-tuple-element.32, f32[]{:T(128)} %get-tuple-element.33), channel_id=1, replica_groups=mesh['term'=8,'sector_0'=4,'sector_1'=4,'sector_2'=2] {'sector_1'}, use_global_device_ids=true, to_apply=%region_26.28 | all-reduce | flops 2 | bytes 16 | tf_op jit(solution)/shard_map/psum | solution.py:52
  456.2 35.5 %all-gather.2.cloned.1.call-done = f32[512,1024]{1,0:T(8,128)} async-done(((f32[64,1024]{1,0:T(8,128)}), f32[512,1024]{1,0:T(8,128)}) %all-gather.2.cloned.1.call-update) | async-done | bytes 2097168 | tf_op jit(solution)/shard_map/all_gather | solution.py:58
  (138 shorter events, 148.1 us)
Async XLA Ops:
  9.3 23.6 %all-to-all-start = ((bf16[32,1,128,128]{3,2,1,0:T(8,128)(2,1)}), bf16[32,1,128,128]{3,2,1,0:T(8,128)(2,1)S(1)}, u32[]{:S(2)}, u32[]{:S(2)}) async-start(bf16[32,1,128,128]{3,2,1,0:T(8,128)(2,1)} %broadcast_in_dim.20), calls=%async_computation | async-start | bytes 2097152 | tf_op jit(solution)/shard_map/all_to_all | solution.py:22
  34.8 37.7 %all-to-all-start.1 = ((f32[8,64,512]{2,1,0:T(8,128)}), f32[8,64,512]{2,1,0:T(8,128)S(1)}, u32[]{:S(2)}, u32[]{:S(2)}) async-start(f32[8,64,512]{2,1,0:T(8,128)} %fusion.40), calls=%async_computation.1 | async-start | bytes 2097152 | tf_op jit(solution)/shard_map/all_to_all | solution.py:46
  43.2 448.5 %all-gather.2.cloned.1.call-start = ((), (), s32[]{:S(2)}) async-start(), calls=%async_computation.5 | async-start | bytes 2359296 | tf_op jit(solution)/shard_map/all_gather | solution.py:58
  72.6 6.7 %collective-permute-start = (f32[64,512]{1,0:T(8,128)S(1)}, f32[64,512]{1,0:T(8,128)S(1)}, u32[]{:S(2)}, u32[]{:S(2)}) collective-permute-start(f32[64,512]{1,0:T(8,128)S(1)} %fusion.39), channel_id=1, source_target_pairs={{0,32},{32,64},{64,96},{96,128},{128,160},{160,192},{192,224},{224... | collective-permute-start | bytes 393224 | tf_op jit(solution)/shard_map/ppermute | solution.py:103
  79.3 6.2 %collective-permute-start.1 = (f32[64,512]{1,0:T(8,128)S(1)}, f32[64,512]{1,0:T(8,128)S(1)}, u32[]{:S(2)}, u32[]{:S(2)}) collective-permute-start(f32[64,512]{1,0:T(8,128)S(1)} %collective-permute-done), channel_id=1, source_target_pairs={{0,32},{32,64},{64,96},{96,128},{128,160},{160,192},{192,224},{224... | collective-permute-start | bytes 393224 | tf_op jit(solution)/shard_map/ppermute | solution.py:103
  79.4 6.2 %collective-permute-start.4 = (f32[64,512]{1,0:T(8,128)S(1)}, f32[64,512]{1,0:T(8,128)S(1)}, u32[]{:S(2)}, u32[]{:S(2)}) collective-permute-start(f32[64,512]{1,0:T(8,128)S(1)} %fusion.39), channel_id=1, source_target_pairs={{0,224},{32,0},{64,32},{96,64},{128,96},{160,128},{192,160},{224,1... | collective-permute-start | bytes 393224 | tf_op jit(solution)/shard_map/ppermute | solution.py:105
  85.5 6.2 %collective-permute-start.2 = (f32[64,512]{1,0:T(8,128)S(1)}, f32[64,512]{1,0:T(8,128)S(1)}, u32[]{:S(2)}, u32[]{:S(2)}) collective-permute-start(f32[64,512]{1,0:T(8,128)S(1)} %collective-permute-done.1), channel_id=1, source_target_pairs={{0,32},{32,64},{64,96},{96,128},{128,160},{160,192},{192,224},{224... | collective-permute-start | bytes 393224 | tf_op jit(solution)/shard_map/ppermute | solution.py:103
  85.5 6.2 %collective-permute-start.5 = (f32[64,512]{1,0:T(8,128)S(1)}, f32[64,512]{1,0:T(8,128)S(1)}, u32[]{:S(2)}, u32[]{:S(2)}) collective-permute-start(f32[64,512]{1,0:T(8,128)S(1)} %collective-permute-done.4), channel_id=1, source_target_pairs={{0,224},{32,0},{64,32},{96,64},{128,96},{160,128},{192,160},{224,1... | collective-permute-start | bytes 393224 | tf_op jit(solution)/shard_map/ppermute | solution.py:105
  91.7 6.2 %collective-permute-start.3 = (f32[64,512]{1,0:T(8,128)S(1)}, f32[64,512]{1,0:T(8,128)S(1)}, u32[]{:S(2)}, u32[]{:S(2)}) collective-permute-start(f32[64,512]{1,0:T(8,128)S(1)} %collective-permute-done.2), channel_id=1, source_target_pairs={{0,32},{32,64},{64,96},{96,128},{128,160},{160,192},{192,224},{224... | collective-permute-start | bytes 393224 | tf_op jit(solution)/shard_map/ppermute | solution.py:103
  91.7 6.4 %collective-permute-start.6 = (f32[64,512]{1,0:T(8,128)S(1)}, f32[64,512]{1,0:T(8,128)S(1)}, u32[]{:S(2)}, u32[]{:S(2)}) collective-permute-start(f32[64,512]{1,0:T(8,128)S(1)} %collective-permute-done.5), channel_id=1, source_target_pairs={{0,224},{32,0},{64,32},{96,64},{128,96},{160,128},{192,160},{224,1... | collective-permute-start | bytes 393224 | tf_op jit(solution)/shard_map/ppermute | solution.py:105
  98.5 16.4 %collective-permute-start.7 = (f32[512,512]{1,0:T(8,128)S(1)}, f32[512,512]{1,0:T(8,128)S(1)}, u32[]{:S(2)}, u32[]{:S(2)}) collective-permute-start(f32[512,512]{1,0:T(8,128)S(1)} %fusion.5), channel_id=1, source_target_pairs={{1,0},{2,1},{3,2},{4,3},{5,4},{6,5},{7,6},{8,7},{9,8},{10,9},{11,1... | collective-permute-start | bytes 3145736 | tf_op jit(solution)/shard_map/ppermute | solution.py:17
  106.2 16.2 %collective-permute-start.8 = (f32[512,512]{1,0:T(8,128)S(1)}, f32[512,512]{1,0:T(8,128)S(1)}, u32[]{:S(2)}, u32[]{:S(2)}) collective-permute-start(f32[512,512]{1,0:T(8,128)S(1)} %fusion.12), channel_id=1, source_target_pairs={{0,1},{1,2},{2,3},{3,4},{4,5},{5,6},{6,7},{7,8},{8,9},{9,10},{10,1... | collective-permute-start | bytes 3145736 | tf_op jit(solution)/shard_map/ppermute | solution.py:17
  197.0 6.9 %collective-permute-start.9 = (f32[64,512]{1,0:T(8,128)S(1)}, f32[64,512]{1,0:T(8,128)S(1)}, u32[]{:S(2)}, u32[]{:S(2)}) collective-permute-start(f32[64,512]{1,0:T(8,128)S(1)} %multiply_subtract_fusion.2), channel_id=1, source_target_pairs={{0,32},{32,64},{64,96},{96,128},{128,160},{160,192},{192,224},{224... | collective-permute-start | bytes 393224 | tf_op jit(solution)/shard_map/ppermute | solution.py:103
  203.8 6.6 %collective-permute-start.10 = (f32[64,512]{1,0:T(8,128)S(1)}, f32[64,512]{1,0:T(8,128)S(1)}, u32[]{:S(2)}, u32[]{:S(2)}) collective-permute-start(f32[64,512]{1,0:T(8,128)S(1)} %collective-permute-done.9), channel_id=1, source_target_pairs={{0,32},{32,64},{64,96},{96,128},{128,160},{160,192},{192,224},{224... | collective-permute-start | bytes 393224 | tf_op jit(solution)/shard_map/ppermute | solution.py:103
  210.4 6.2 %collective-permute-start.11 = (f32[64,512]{1,0:T(8,128)S(1)}, f32[64,512]{1,0:T(8,128)S(1)}, u32[]{:S(2)}, u32[]{:S(2)}) collective-permute-start(f32[64,512]{1,0:T(8,128)S(1)} %collective-permute-done.10), channel_id=1, source_target_pairs={{0,32},{32,64},{64,96},{96,128},{128,160},{160,192},{192,224},{224... | collective-permute-start | bytes 393224 | tf_op jit(solution)/shard_map/ppermute | solution.py:103
  216.6 6.2 %collective-permute-start.12 = (f32[64,512]{1,0:T(8,128)S(1)}, f32[64,512]{1,0:T(8,128)S(1)}, u32[]{:S(2)}, u32[]{:S(2)}) collective-permute-start(f32[64,512]{1,0:T(8,128)S(1)} %collective-permute-done.11), channel_id=1, source_target_pairs={{0,32},{32,64},{64,96},{96,128},{128,160},{160,192},{192,224},{224... | collective-permute-start | bytes 393224 | tf_op jit(solution)/shard_map/ppermute | solution.py:103
  216.6 6.3 %collective-permute-start.15 = (f32[64,512]{1,0:T(8,128)S(1)}, f32[64,512]{1,0:T(8,128)S(1)}, u32[]{:S(2)}, u32[]{:S(2)}) collective-permute-start(f32[64,512]{1,0:T(8,128)S(1)} %collective-permute-done.14), channel_id=1, source_target_pairs={{0,224},{32,0},{64,32},{96,64},{128,96},{160,128},{192,160},{224,1... | collective-permute-start | bytes 393224 | tf_op jit(solution)/shard_map/ppermute | solution.py:105
  225.2 14.2 %collective-permute-start.16 = (f32[512,512]{1,0:T(8,128)S(1)}, f32[512,512]{1,0:T(8,128)S(1)}, u32[]{:S(2)}, u32[]{:S(2)}) collective-permute-start(f32[512,512]{1,0:T(8,128)S(1)} %fusion.4), channel_id=1, source_target_pairs={{1,0},{2,1},{3,2},{4,3},{5,4},{6,5},{7,6},{8,7},{9,8},{10,9},{11,1... | collective-permute-start | bytes 3145736 | tf_op jit(solution)/shard_map/ppermute | solution.py:17
  230.6 16.8 %collective-permute-start.17 = (f32[512,512]{1,0:T(8,128)S(1)}, f32[512,512]{1,0:T(8,128)S(1)}, u32[]{:S(2)}, u32[]{:S(2)}) collective-permute-start(f32[512,512]{1,0:T(8,128)S(1)} %fusion.9), channel_id=1, source_target_pairs={{0,1},{1,2},{2,3},{3,4},{4,5},{5,6},{6,7},{7,8},{8,9},{9,10},{10,1... | collective-permute-start | bytes 3145736 | tf_op jit(solution)/shard_map/ppermute | solution.py:17
  328.4 7.0 %collective-permute-start.18 = (f32[64,512]{1,0:T(8,128)S(1)}, f32[64,512]{1,0:T(8,128)S(1)}, u32[]{:S(2)}, u32[]{:S(2)}) collective-permute-start(f32[64,512]{1,0:T(8,128)S(1)} %get-tuple-element.44), channel_id=1, source_target_pairs={{0,32},{32,64},{64,96},{96,128},{128,160},{160,192},{192,224},{224... | collective-permute-start | bytes 393224 | tf_op jit(solution)/shard_map/ppermute | solution.py:103
  335.4 6.2 %collective-permute-start.19 = (f32[64,512]{1,0:T(8,128)S(1)}, f32[64,512]{1,0:T(8,128)S(1)}, u32[]{:S(2)}, u32[]{:S(2)}) collective-permute-start(f32[64,512]{1,0:T(8,128)S(1)} %collective-permute-done.18), channel_id=1, source_target_pairs={{0,32},{32,64},{64,96},{96,128},{128,160},{160,192},{192,224},{224... | collective-permute-start | bytes 393224 | tf_op jit(solution)/shard_map/ppermute | solution.py:103
  347.8 6.3 %collective-permute-start.24 = (f32[64,512]{1,0:T(8,128)S(1)}, f32[64,512]{1,0:T(8,128)S(1)}, u32[]{:S(2)}, u32[]{:S(2)}) collective-permute-start(f32[64,512]{1,0:T(8,128)S(1)} %collective-permute-done.23), channel_id=1, source_target_pairs={{0,224},{32,0},{64,32},{96,64},{128,96},{160,128},{192,160},{224,1... | collective-permute-start | bytes 393224 | tf_op jit(solution)/shard_map/ppermute | solution.py:105
  356.4 14.2 %collective-permute-start.25 = (f32[512,512]{1,0:T(8,128)S(1)}, f32[512,512]{1,0:T(8,128)S(1)}, u32[]{:S(2)}, u32[]{:S(2)}) collective-permute-start(f32[512,512]{1,0:T(8,128)S(1)} %fusion.3), channel_id=1, source_target_pairs={{1,0},{2,1},{3,2},{4,3},{5,4},{6,5},{7,6},{8,7},{9,8},{10,9},{11,1... | collective-permute-start | bytes 3145736 | tf_op jit(solution)/shard_map/ppermute | solution.py:17
  361.8 16.9 %collective-permute-start.26 = (f32[512,512]{1,0:T(8,128)S(1)}, f32[512,512]{1,0:T(8,128)S(1)}, u32[]{:S(2)}, u32[]{:S(2)}) collective-permute-start(f32[512,512]{1,0:T(8,128)S(1)} %fusion.6), channel_id=1, source_target_pairs={{0,1},{1,2},{2,3},{3,4},{4,5},{5,6},{6,7},{7,8},{8,9},{9,10},{10,1... | collective-permute-start | bytes 3145736 | tf_op jit(solution)/shard_map/ppermute | solution.py:17
  (17 other events, 344.3 us)
Sparse Core Ops, SparseCore 0:
  456.4 35.3 all-gather.1
